TPU v7x, 32 devices: a whole 2x2x4 slice. The times are simulated.
32 devices in a mesh: dp: 16 (over z, y, core), fsdp: 2 (over x).
Axes of the slice: x: 2, y: 2, z: 4, core: 2. Of those that a mesh axis runs over, the one named last changes fastest.
Arguments:
- hidden_in: bfloat16 [4096, 1024], P(('dp', 'fsdp')), may hold values from -6 to 6
- doc_id: int32 [4096], P(('dp', 'fsdp')), may hold values from 0 to 128, as said below
- expert_ids: int32 [4096, 8], P(('dp', 'fsdp')), may hold values from 0 to 15, all different within a row
- out_grad: bfloat16 [4096, 1024], P(('dp', 'fsdp')), may hold values from -6 to 6
- attn_gain: bfloat16 [1024], P(('dp', 'fsdp')), may hold values from 0.5 to 1.5
- query_weight: bfloat16 [1024, 1024], P(('dp', 'fsdp')), may hold values from -0.1875 to 0.1875
- key_weight: bfloat16 [1024, 512], P(('dp', 'fsdp')), may hold values from -0.1875 to 0.1875
- value_weight: bfloat16 [1024, 512], P(('dp', 'fsdp')), may hold values from -0.1875 to 0.1875
- output_weight: bfloat16 [1024, 1024], P(('dp', 'fsdp')), may hold values from -0.75 to 0.75
- ffn_gain: bfloat16 [1024], P(('dp', 'fsdp')), may hold values from 0.5 to 1.5
- router_weight: bfloat16 [1024, 16], P(('dp', 'fsdp')), may hold values from -0.375 to 0.375
- expert_gate: bfloat16 [16, 1024, 512], P('dp', 'fsdp'), may hold values from -0.1875 to 0.1875
- expert_up: bfloat16 [16, 1024, 512], P('dp', 'fsdp'), may hold values from -0.1875 to 0.1875
- expert_down: bfloat16 [16, 512, 1024], P('dp', 'fsdp'), may hold values from -1 to 1
Outputs:
- layer_out: bfloat16 [4096, 1024], P(('dp', 'fsdp'))
- grad_in: bfloat16 [4096, 1024], P(('dp', 'fsdp'))
- grad_attn_gain: float32 [1024], P(('dp', 'fsdp'))
- grad_query: float32 [1024, 1024], P(('dp', 'fsdp'))
- grad_key: float32 [1024, 512], P(('dp', 'fsdp'))
- grad_value: float32 [1024, 512], P(('dp', 'fsdp'))
- grad_output: float32 [1024, 1024], P(('dp', 'fsdp'))
- grad_ffn_gain: float32 [1024], P(('dp', 'fsdp'))
- grad_router: float32 [1024, 16], P(('dp', 'fsdp'))
- grad_expert_gate: float32 [16, 1024, 512], P('dp', 'fsdp')
- grad_expert_up: float32 [16, 1024, 512], P('dp', 'fsdp')
- grad_expert_down: float32 [16, 512, 1024], P('dp', 'fsdp')
Inputs may be any that keep to these rules, and one draw needn't show every extreme that they name: Within each block of 128 rows doc_id starts at 0 and never falls; live rows come first and carry ids below 128; the rows after them carry 128 (padding). Every block has 64 or more live rows and some block has no padding. `expert_ids`: each row names 8 different experts.
All inputs are finite; a program needn't handle non-finite values.
Results may differ from a plain program's by a relative error of at most 0.015.
The roundings to bfloat16 on the way count: a program that leaves them out, or rounds other values in their place, can miss the bound.
Values may be sent and summed in bfloat16 or wider, within the bound.
A program may use at most 128 MiB of HBM per device.

v0:
```python
import jax
import jax.numpy as jnp
from jax import lax
from jax.sharding import PartitionSpec as P

HEADS = 16
KV_HEADS = 8
HEAD_DIM = 64
TOP = 8
CAP = 24
norm_eps = 1e-05


def positions_mask(doc_block):
    row_count = doc_block.shape[0]
    row_index = jnp.arange(row_count)
    same_doc = doc_block[:, None] == doc_block[None, :]
    earlier = row_index[None, :] < row_index[:, None]
    position = jnp.sum((same_doc & earlier).astype(jnp.float32), axis=1)
    allowed = same_doc & (row_index[None, :] <= row_index[:, None])
    live_rows = (doc_block < row_count).astype(jnp.float32)
    return (position, allowed, live_rows)


def rope_tables(position):
    half_dim = HEAD_DIM // 2
    freqs = jnp.exp(-jnp.log(10000.0) * (2.0 * jnp.arange(half_dim, dtype=jnp.float32) / HEAD_DIM))
    angle = position[:, None] * freqs[None, :]
    return (jnp.cos(angle), jnp.sin(angle))


def rotate(values, cosine, sinusoid):
    half_dim = values.shape[-1] // 2
    first_half, second_half = (values[..., :half_dim], values[..., half_dim:])
    return jnp.concatenate(
        [
            first_half * cosine - second_half * sinusoid,
            second_half * cosine + first_half * sinusoid,
        ],
        axis=-1,
    )


def unrotate(values, cosine, sinusoid):
    half_dim = values.shape[-1] // 2
    first_half, second_half = (values[..., :half_dim], values[..., half_dim:])
    return jnp.concatenate(
        [
            first_half * cosine + second_half * sinusoid,
            second_half * cosine - first_half * sinusoid,
        ],
        axis=-1,
    )


def norm_forward(values, gain):
    scale_row = lax.rsqrt(jnp.mean(values * values, axis=-1, keepdims=True) + norm_eps)
    normed = values * scale_row
    return (normed, scale_row, (normed * gain).astype(jnp.bfloat16))


def norm_backward(upstream, normed, scale_row, gain):
    scaled = upstream * gain
    inner = jnp.mean(scaled * normed, axis=-1, keepdims=True)
    return (scale_row * (scaled - normed * inner), jnp.sum(upstream * normed, axis=0))


def probabilities(query_b, key_b, allowed, log_total):
    scores = jnp.einsum(
        "ikgd,jkd->kgij", query_b, key_b, preferred_element_type=jnp.float32
    ) * HEAD_DIM ** (-0.5)
    raised = jnp.where(allowed[None, None], jnp.exp(scores), 0.0)
    if log_total is None:
        log_total = jnp.log(jnp.sum(raised, axis=-1, keepdims=True))
    return (jnp.where(allowed[None, None], jnp.exp(scores - log_total), 0.0), log_total)


def routing(expert_block, live_rows, logits):
    experts = logits.shape[1]
    row_count = expert_block.shape[0]
    chosen = jnp.sum(
        (expert_block[:, :, None] == jnp.arange(experts)[None, None, :]).astype(jnp.float32), axis=1
    )
    raised = jnp.where(chosen > 0, jnp.exp(logits), 0.0)
    gates = raised / jnp.sum(raised, axis=1, keepdims=True)
    member = chosen * live_rows[:, None]
    lower = (jnp.arange(row_count)[None, :] < jnp.arange(row_count)[:, None]).astype(jnp.float32)
    rank = jnp.dot(lower, member, precision=lax.Precision.HIGHEST)
    kept = member * (rank < CAP).astype(jnp.float32)
    slot_match = (rank.T[:, None, :] == jnp.arange(CAP, dtype=jnp.float32)[None, :, None]).astype(
        jnp.float32
    )
    dispatch = kept.T[:, None, :] * slot_match
    return (gates, dispatch, kept, rank)


def expert_forward(rows_in, w_gate, w_up, w_down):
    gate_pre = jnp.dot(rows_in, w_gate, preferred_element_type=jnp.float32)
    up_pre = jnp.dot(rows_in, w_up, preferred_element_type=jnp.float32)
    act_rows = (jax.nn.silu(gate_pre) * up_pre).astype(jnp.bfloat16)
    out_rows = jnp.dot(act_rows, w_down, preferred_element_type=jnp.float32).astype(jnp.bfloat16)
    return (gate_pre, up_pre, act_rows, out_rows)


def expert_backward(rows_in, gate_pre, up_pre, act_rows, grad_rows, w_gate, w_up, w_down):
    grad_act = jnp.dot(grad_rows, w_down.T, preferred_element_type=jnp.float32)
    sigmoid_gate = jax.nn.sigmoid(gate_pre)
    grad_up_pre = (grad_act * gate_pre * sigmoid_gate).astype(jnp.bfloat16)
    grad_gate_pre = (
        grad_act * up_pre * sigmoid_gate * (1.0 + gate_pre * (1.0 - sigmoid_gate))
    ).astype(jnp.bfloat16)
    grad_down_w = jnp.dot(act_rows.T, grad_rows, preferred_element_type=jnp.float32)
    grad_gate_w = jnp.dot(rows_in.T, grad_gate_pre, preferred_element_type=jnp.float32)
    grad_up_w = jnp.dot(rows_in.T, grad_up_pre, preferred_element_type=jnp.float32)
    grad_rows_in = jnp.dot(grad_gate_pre, w_gate.T, preferred_element_type=jnp.float32)
    grad_rows_in = (
        grad_rows_in + jnp.dot(grad_up_pre, w_up.T, preferred_element_type=jnp.float32)
    ).astype(jnp.bfloat16)
    return (grad_rows_in, grad_gate_w, grad_up_w, grad_down_w)


def shards(
    hidden_in,
    doc_id,
    expert_ids,
    out_grad,
    attn_gain,
    query_weight,
    key_weight,
    value_weight,
    output_weight,
    ffn_gain,
    router_weight,
    expert_gate,
    expert_up,
    expert_down,
):
    rows = hidden_in.shape[0]
    groups = HEADS // KV_HEADS
    scale = HEAD_DIM ** (-0.5)
    dense_full = (
        lax.all_gather(attn_gain, ("dp", "fsdp"), axis=0, tiled=True),
        lax.all_gather(query_weight, ("dp", "fsdp"), axis=0, tiled=True),
        lax.all_gather(key_weight, ("dp", "fsdp"), axis=0, tiled=True),
        lax.all_gather(value_weight, ("dp", "fsdp"), axis=0, tiled=True),
        lax.all_gather(output_weight, ("dp", "fsdp"), axis=0, tiled=True),
        lax.all_gather(ffn_gain, ("dp", "fsdp"), axis=0, tiled=True),
        lax.all_gather(router_weight, ("dp", "fsdp"), axis=0, tiled=True),
    )
    expert_full = (
        lax.all_gather(expert_gate, "fsdp", axis=1, tiled=True),
        lax.all_gather(expert_up, "fsdp", axis=1, tiled=True),
        lax.all_gather(expert_down, "fsdp", axis=1, tiled=True),
    )
    gain_one, w_query, w_key, w_value, w_output, gain_two, w_router = dense_full
    w_gate, w_up, w_down = (expert_full[0][0], expert_full[1][0], expert_full[2][0])
    position, allowed, live_rows = positions_mask(doc_id)
    cosine, sinusoid = rope_tables(position)
    cos_query, sin_query = (cosine[:, None, None, :], sinusoid[:, None, None, :])
    cos_key, sin_key = (cosine[:, None, :], sinusoid[:, None, :])
    resid_in = hidden_in.astype(jnp.float32)
    normed_one, scale_one, normed_in = norm_forward(resid_in, gain_one.astype(jnp.float32))
    query_raw = jnp.dot(normed_in, w_query, preferred_element_type=jnp.float32).reshape(
        rows, KV_HEADS, groups, HEAD_DIM
    )
    key_raw = jnp.dot(normed_in, w_key, preferred_element_type=jnp.float32).reshape(
        rows, KV_HEADS, HEAD_DIM
    )
    query_b = rotate(query_raw, cos_query, sin_query).astype(jnp.bfloat16)
    key_b = rotate(key_raw, cos_key, sin_key).astype(jnp.bfloat16)
    value_b = (
        jnp.dot(normed_in, w_value, preferred_element_type=jnp.float32)
        .reshape(rows, KV_HEADS, HEAD_DIM)
        .astype(jnp.bfloat16)
    )
    probs, log_total = probabilities(query_b, key_b, allowed, None)
    probs_b = probs.astype(jnp.bfloat16)
    mixed = jnp.einsum("kgij,jkd->ikgd", probs_b, value_b, preferred_element_type=jnp.float32)
    mixed_b = (
        (mixed * live_rows[:, None, None, None])
        .reshape(rows, HEADS * HEAD_DIM)
        .astype(jnp.bfloat16)
    )
    resid_mid = resid_in + jnp.dot(mixed_b, w_output, preferred_element_type=jnp.float32)
    normed_two, scale_two, routed_in = norm_forward(resid_mid, gain_two.astype(jnp.float32))
    logits = jnp.dot(routed_in, w_router, preferred_element_type=jnp.float32)
    gates, dispatch, kept, rank = routing(expert_ids, live_rows, logits)
    dispatch_b = dispatch.astype(jnp.bfloat16)
    send_rows = jnp.einsum(
        "ecr,rd->ecd", dispatch_b, routed_in, preferred_element_type=jnp.float32
    ).astype(jnp.bfloat16)
    recv_rows = lax.all_to_all(send_rows, "dp", split_axis=0, concat_axis=0, tiled=True)
    flat_in = recv_rows.reshape(-1, recv_rows.shape[2])
    gate_pre, up_pre, act_rows, out_rows = expert_forward(flat_in, w_gate, w_up, w_down)
    back_rows = lax.all_to_all(
        out_rows.reshape(recv_rows.shape), "dp", split_axis=0, concat_axis=0, tiled=True
    )
    experts = back_rows.shape[0]
    capacity = back_rows.shape[1]
    width = back_rows.shape[2]
    chosen_slot = (expert_ids[:, :, None] == jnp.arange(experts)[None, None, :]).astype(jnp.float32)
    gate_pick = jnp.sum(chosen_slot * (gates * kept)[:, None, :], axis=2)
    rank_pick = jnp.sum(chosen_slot * rank[:, None, :], axis=2)
    slot_index = expert_ids * capacity + jnp.minimum(rank_pick, capacity - 1.0).astype(jnp.int32)
    back_flat = back_rows.reshape(experts * capacity, width)
    picked_rows = jnp.take(back_flat, slot_index.reshape(-1), axis=0).reshape(rows, TOP, width)
    expert_sum = jnp.sum(gate_pick[:, :, None] * picked_rows.astype(jnp.float32), axis=1)
    layer_out = (resid_mid + expert_sum).astype(jnp.bfloat16)
    dense_full = (
        lax.all_gather(attn_gain, ("dp", "fsdp"), axis=0, tiled=True),
        lax.all_gather(query_weight, ("dp", "fsdp"), axis=0, tiled=True),
        lax.all_gather(key_weight, ("dp", "fsdp"), axis=0, tiled=True),
        lax.all_gather(value_weight, ("dp", "fsdp"), axis=0, tiled=True),
        lax.all_gather(output_weight, ("dp", "fsdp"), axis=0, tiled=True),
        lax.all_gather(ffn_gain, ("dp", "fsdp"), axis=0, tiled=True),
        lax.all_gather(router_weight, ("dp", "fsdp"), axis=0, tiled=True),
    )
    expert_full = (
        lax.all_gather(expert_gate, "fsdp", axis=1, tiled=True),
        lax.all_gather(expert_up, "fsdp", axis=1, tiled=True),
        lax.all_gather(expert_down, "fsdp", axis=1, tiled=True),
    )
    gain_one, w_query, w_key, w_value, w_output, gain_two, w_router = dense_full
    w_gate, w_up, w_down = (expert_full[0][0], expert_full[1][0], expert_full[2][0])
    grad_out = out_grad.astype(jnp.float32)
    slot_gate = jnp.sum(dispatch * gates.T[:, None, :], axis=2)
    pulled_grad = jnp.einsum(
        "ecr,rd->ecd", dispatch_b, out_grad, preferred_element_type=jnp.float32
    )
    grad_send = (slot_gate[:, :, None] * pulled_grad).astype(jnp.bfloat16)
    slot_dot = jnp.sum(back_rows.astype(jnp.float32) * pulled_grad, axis=2)
    grad_gates = jnp.sum(dispatch * slot_dot[:, :, None], axis=1).T
    grad_logits = gates * (grad_gates - jnp.sum(gates * grad_gates, axis=1, keepdims=True))
    grad_logits_b = grad_logits.astype(jnp.bfloat16)
    grad_recv = lax.all_to_all(grad_send, "dp", split_axis=0, concat_axis=0, tiled=True)
    grad_rows_in, grad_gate_w, grad_up_w, grad_down_w = expert_backward(
        flat_in, gate_pre, up_pre, act_rows, grad_recv.reshape(flat_in.shape), w_gate, w_up, w_down
    )
    grad_back = lax.all_to_all(
        grad_rows_in.reshape(recv_rows.shape), "dp", split_axis=0, concat_axis=0, tiled=True
    )
    grad_routed = jnp.einsum(
        "ecr,ecd->rd", dispatch_b, grad_back, preferred_element_type=jnp.float32
    )
    grad_routed = grad_routed + jnp.dot(
        grad_logits_b, w_router.T, preferred_element_type=jnp.float32
    )
    grad_w_router = jnp.dot(routed_in.T, grad_logits_b, preferred_element_type=jnp.float32)
    grad_norm_two, grad_gain_two = norm_backward(
        grad_routed, normed_two, scale_two, gain_two.astype(jnp.float32)
    )
    grad_mid = grad_out + grad_norm_two
    grad_mid_b = grad_mid.astype(jnp.bfloat16)
    grad_w_output = jnp.dot(mixed_b.T, grad_mid_b, preferred_element_type=jnp.float32)
    grad_mixed = jnp.dot(grad_mid_b, w_output.T, preferred_element_type=jnp.float32).reshape(
        rows, KV_HEADS, groups, HEAD_DIM
    )
    grad_mixed = (grad_mixed * live_rows[:, None, None, None]).astype(jnp.bfloat16)
    probs_again, unused_total = probabilities(query_b, key_b, allowed, log_total)
    grad_probs = jnp.einsum(
        "ikgd,jkd->kgij", grad_mixed, value_b, preferred_element_type=jnp.float32
    )
    delta = jnp.sum(probs_again * grad_probs, axis=-1, keepdims=True)
    grad_scores = (probs_again * (grad_probs - delta) * scale).astype(jnp.bfloat16)
    grad_query_raw = jnp.einsum(
        "kgij,jkd->ikgd", grad_scores, key_b, preferred_element_type=jnp.float32
    )
    grad_key_raw = jnp.einsum(
        "kgij,ikgd->jkd", grad_scores, query_b, preferred_element_type=jnp.float32
    )
    grad_value_raw = jnp.einsum(
        "kgij,ikgd->jkd",
        probs_again.astype(jnp.bfloat16),
        grad_mixed,
        preferred_element_type=jnp.float32,
    )
    grad_query_b = (
        unrotate(grad_query_raw, cos_query, sin_query)
        .reshape(rows, HEADS * HEAD_DIM)
        .astype(jnp.bfloat16)
    )
    grad_key_b = (
        unrotate(grad_key_raw, cos_key, sin_key)
        .reshape(rows, KV_HEADS * HEAD_DIM)
        .astype(jnp.bfloat16)
    )
    grad_value_b = grad_value_raw.reshape(rows, KV_HEADS * HEAD_DIM).astype(jnp.bfloat16)
    grad_w_query = jnp.dot(normed_in.T, grad_query_b, preferred_element_type=jnp.float32)
    grad_w_key = jnp.dot(normed_in.T, grad_key_b, preferred_element_type=jnp.float32)
    grad_w_value = jnp.dot(normed_in.T, grad_value_b, preferred_element_type=jnp.float32)
    grad_normed = jnp.dot(grad_query_b, w_query.T, preferred_element_type=jnp.float32)
    grad_normed = grad_normed + jnp.dot(grad_key_b, w_key.T, preferred_element_type=jnp.float32)
    grad_normed = grad_normed + jnp.dot(grad_value_b, w_value.T, preferred_element_type=jnp.float32)
    grad_norm_one, grad_gain_one = norm_backward(
        grad_normed, normed_one, scale_one, gain_one.astype(jnp.float32)
    )
    grad_input = (grad_mid + grad_norm_one).astype(jnp.bfloat16)
    dense_grads = (
        lax.psum_scatter(grad_gain_one, ("dp", "fsdp"), scatter_dimension=0, tiled=True),
        lax.psum_scatter(grad_w_query, ("dp", "fsdp"), scatter_dimension=0, tiled=True),
        lax.psum_scatter(grad_w_key, ("dp", "fsdp"), scatter_dimension=0, tiled=True),
        lax.psum_scatter(grad_w_value, ("dp", "fsdp"), scatter_dimension=0, tiled=True),
        lax.psum_scatter(grad_w_output, ("dp", "fsdp"), scatter_dimension=0, tiled=True),
        lax.psum_scatter(grad_gain_two, ("dp", "fsdp"), scatter_dimension=0, tiled=True),
        lax.psum_scatter(grad_w_router, ("dp", "fsdp"), scatter_dimension=0, tiled=True),
    )
    expert_grads = (
        lax.psum_scatter(
            grad_gate_w[None].astype(jnp.bfloat16), "fsdp", scatter_dimension=1, tiled=True
        ).astype(jnp.float32),
        lax.psum_scatter(
            grad_up_w[None].astype(jnp.bfloat16), "fsdp", scatter_dimension=1, tiled=True
        ).astype(jnp.float32),
        lax.psum_scatter(
            grad_down_w[None].astype(jnp.bfloat16), "fsdp", scatter_dimension=1, tiled=True
        ).astype(jnp.float32),
    )
    return (
        layer_out,
        grad_input,
        dense_grads[0],
        dense_grads[1],
        dense_grads[2],
        dense_grads[3],
        dense_grads[4],
        dense_grads[5],
        dense_grads[6],
        expert_grads[0],
        expert_grads[1],
        expert_grads[2],
    )


def solution(mesh):
    in_specs = (
        P(("dp", "fsdp"), None),
        P(("dp", "fsdp")),
        P(("dp", "fsdp"), None),
        P(("dp", "fsdp"), None),
        P(("dp", "fsdp")),
        P(("dp", "fsdp"), None),
        P(("dp", "fsdp"), None),
        P(("dp", "fsdp"), None),
        P(("dp", "fsdp"), None),
        P(("dp", "fsdp")),
        P(("dp", "fsdp"), None),
        P("dp", "fsdp", None),
        P("dp", "fsdp", None),
        P("dp", "fsdp", None),
    )
    out_specs = (
        P(("dp", "fsdp"), None),
        P(("dp", "fsdp"), None),
        P(("dp", "fsdp")),
        P(("dp", "fsdp"), None),
        P(("dp", "fsdp"), None),
        P(("dp", "fsdp"), None),
        P(("dp", "fsdp"), None),
        P(("dp", "fsdp")),
        P(("dp", "fsdp"), None),
        P("dp", "fsdp", None),
        P("dp", "fsdp", None),
        P("dp", "fsdp", None),
    )
    return jax.shard_map(shards, mesh=mesh, in_specs=in_specs, out_specs=out_specs, check_vma=False)
```

profile of v0, /device:TPU:0, one launch (start us, length us, event | category | flops | bytes accessed | tf_op | source)
XLA Modules:
  0.0 1174.7 jit_solution(4902561280423588323)
XLA Ops:
  15.2 41.9 %all-reduce.5 = (bf16[1024]{0:T(1024)(128)(2,1)S(1)}, bf16[1024]{0:T(1024)(128)(2,1)S(1)}) all-reduce(bf16[1024]{0:T(1024)(128)(2,1)S(1)} %dynamic-update-slice, bf16[1024]{0:T(1024)(128)(2,1)S(1)} %dynamic-update-slice.1), channel_id=1, replica_groups=mesh['dp'=16,'fsdp'=2] {'dp','fsdp'}, use_global_device_ids=true, to_apply=%add | all-reduce | flops 2048 | bytes 8192
  59.3 8.2 all-gather.9.cloned.1.call-done
  69.3 54.0 %all-gather.11.cloned.1.call-done = bf16[1024,512]{1,0:T(8,128)(2,1)} async-done(((bf16[32,512]{1,0:T(8,128)(2,1)}), bf16[1024,512]{1,0:T(8,128)(2,1)}) %all-gather.11.cloned.1.call-update) | async-done | bytes 1048592 | tf_op jit(solution)/shard_map/all_gather | solution.py:144
  125.1 56.5 %all-gather.13.cloned.1.call-done = bf16[1024,1024]{1,0:T(8,128)(2,1)} async-done(((bf16[32,1024]{1,0:T(8,128)(2,1)}), bf16[1024,1024]{1,0:T(8,128)(2,1)}) %all-gather.13.cloned.1.call-update) | async-done | bytes 2097168 | tf_op jit(solution)/shard_map/all_gather | solution.py:143
  181.6 2.6 fusion.97
  185.5 54.2 %all-gather.15.cloned.1.call-done = bf16[1024,1024]{1,0:T(8,128)(2,1)} async-done(((bf16[32,1024]{1,0:T(8,128)(2,1)}), bf16[1024,1024]{1,0:T(8,128)(2,1)}) %all-gather.15.cloned.1.call-update) | async-done | bytes 2097168 | tf_op jit(solution)/shard_map/all_gather | solution.py:146
  244.0 4.5 all-to-all-start
  249.2 12.0 %all-gather.17.cloned.1.call-done = bf16[1,1024,512]{2,1,0:T(8,128)(2,1)} async-done(((bf16[1,512,512]{2,1,0:T(8,128)(2,1)}), bf16[1,1024,512]{2,1,0:T(8,128)(2,1)}) %all-gather.17.cloned.1.call-update) | async-done | bytes 1048592 | tf_op jit(solution)/shard_map/all_gather | solution.py:151
  261.2 5.9 all-to-all-done
  268.9 15.0 %all-gather.19.cloned.1.call-done = bf16[1,1024,512]{2,1,0:T(8,128)(2,1)} async-done(((bf16[1,512,512]{2,1,0:T(8,128)(2,1)}), bf16[1,1024,512]{2,1,0:T(8,128)(2,1)}) %all-gather.19.cloned.1.call-update) | async-done | bytes 1048592 | tf_op jit(solution)/shard_map/all_gather | solution.py:152
  284.0 2.7 multiply_convert_fusion.3
  286.6 20.2 %all-gather.21.cloned.1.call-done = bf16[1,512,1024]{2,1,0:T(8,128)(2,1)} async-done(((bf16[1,256,1024]{2,1,0:T(8,128)(2,1)}), bf16[1,512,1024]{2,1,0:T(8,128)(2,1)}) %all-gather.21.cloned.1.call-update) | async-done | bytes 1048592 | tf_op jit(solution)/shard_map/all_gather | solution.py:153
  306.8 2.8 convolution_convert_fusion.3
  309.6 5.6 all-to-all-start.1
  315.2 76.2 %all-gather = bf16[32,32,16]{1,2,0:T(8,128)(2,1)S(1)} all-gather(bf16[1,32,16]{1,2,0:T(8,128)(2,1)S(1)} %bitcast.165), channel_id=1, replica_groups=mesh['dp'=16,'fsdp'=2] {'dp','fsdp'}, dimensions={0}, use_global_device_ids=true | all-gather | bytes 33792 | tf_op jit(solution)/shard_map/all_gather | solution.py:148
  393.6 3.6 all-to-all-start.2
  399.0 16.8 %all-to-all-done.2 = bf16[16,24,1024]{2,1,0:T(8,128)(2,1)S(1)} async-done(((bf16[16,24,1024]{2,1,0:T(8,128)(2,1)}), bf16[16,24,1024]{2,1,0:T(8,128)(2,1)S(1)}, u32[]{:S(2)}, u32[]{:S(2)}) %all-to-all-start.2) | async-done | bytes 786464 | tf_op jit(solution)/shard_map/all_to_all | solution.py:235
  415.8 2.8 multiply_convert_fusion.1
  426.2 5.7 all-to-all-start.3
  433.9 4.1 gather_fusion
  438.0 2.3 multiply_reduce_fusion
  442.1 8.6 all-to-all-done.3
  465.8 2.8 fusion.95
  469.6 2.7 fusion.56
  472.3 65.3 %reduce-scatter.25.cloned.1.call-done = f32[32,16]{1,0:T(8,128)} async-done(((f32[1024,16]{1,0:T(8,128)}), f32[32,16]{1,0:T(8,128)}) %reduce-scatter.25.cloned.1.call-update) | async-done | bytes 2064
  541.4 38.1 %all-reduce.4 = (f32[1024]{0:T(1024)S(1)}, f32[1024]{0:T(1024)S(1)}) all-reduce(f32[1024]{0:T(1024)S(1)} %get-tuple-element.14, f32[1024]{0:T(1024)S(1)} %copy-done.49), channel_id=2, replica_groups=mesh['dp'=16,'fsdp'=2] {'dp','fsdp'}, use_global_device_ids=true, to_apply=%region_17.18.clone | all-reduce | flops 2048 | bytes 16384
  581.6 2.1 convert_element_type.188
  585.9 17.1 %reduce-scatter.23.cloned.1.call-done = bf16[1,256,1024]{2,1,0:T(8,128)(2,1)} async-done(((bf16[1,512,1024]{2,1,0:T(8,128)(2,1)}), bf16[1,256,1024]{2,1,0:T(8,128)(2,1)}) %reduce-scatter.23.cloned.1.call-update) | async-done | bytes 524304 | tf_op jit(solution)/shard_map/reduce_scatter | solution.py:314
  605.0 139.8 %reduce-scatter.13.cloned.1.call-done = f32[32,512]{1,0:T(8,128)} async-done(((f32[1024,512]{1,0:T(8,128)}), f32[32,512]{1,0:T(8,128)}) %reduce-scatter.13.cloned.1.call-update) | async-done | bytes 65552 | tf_op jit(solution)/shard_map/reduce_scatter | solution.py:301
  744.9 137.4 %reduce-scatter.15.cloned.1.call-done = f32[32,512]{1,0:T(8,128)} async-done(((f32[1024,512]{1,0:T(8,128)}), f32[32,512]{1,0:T(8,128)}) %reduce-scatter.15.cloned.1.call-update) | async-done | bytes 65552 | tf_op jit(solution)/shard_map/reduce_scatter | solution.py:302
  882.3 142.9 %reduce-scatter.11.cloned.1.call-done = f32[32,1024]{1,0:T(8,128)} async-done(((f32[1024,1024]{1,0:T(8,128)}), f32[32,1024]{1,0:T(8,128)}) %reduce-scatter.11.cloned.1.call-update) | async-done | bytes 131088 | tf_op jit(solution)/shard_map/reduce_scatter | solution.py:300
  1025.2 143.0 %reduce-scatter.17.cloned.1.call-done = f32[32,1024]{1,0:T(8,128)} async-done(((f32[1024,1024]{1,0:T(8,128)}), f32[32,1024]{1,0:T(8,128)}) %reduce-scatter.17.cloned.1.call-update) | async-done | bytes 131088 | tf_op jit(solution)/shard_map/reduce_scatter | solution.py:303
  (223 shorter events, 62.7 us)
Async XLA Ops:
  7.2 116.1 %copy-start = (bf16[128,1024]{1,0:T(8,128)(2,1)S(1)}, bf16[128,1024]{1,0:T(8,128)(2,1)}, u32[]{:S(2)}) copy-start(bf16[128,1024]{1,0:T(8,128)(2,1)} %param.14) | copy-start | bytes 786436
  7.2 60.3 %all-gather.9.cloned.1.call-start = ((), (), s32[]{:S(2)}) async-start(), calls=%async_computation.12 | async-start | bytes 1081344 | tf_op jit(solution)/shard_map/all_gather | solution.py:145
  7.9 115.3 %all-gather.11.cloned.1.call-start = ((), (), s32[]{:S(2)}) async-start(), calls=%async_computation.13 | async-start | bytes 1081344 | tf_op jit(solution)/shard_map/all_gather | solution.py:144
  8.7 172.9 %all-gather.13.cloned.1.call-start = ((), (), s32[]{:S(2)}) async-start(), calls=%async_computation.14 | async-start | bytes 2162688 | tf_op jit(solution)/shard_map/all_gather | solution.py:143
  9.4 230.3 %all-gather.15.cloned.1.call-start = ((), (), s32[]{:S(2)}) async-start(), calls=%async_computation.15 | async-start | bytes 2162688 | tf_op jit(solution)/shard_map/all_gather | solution.py:146
  10.0 251.3 %all-gather.17.cloned.1.call-start = ((), (), s32[]{:S(2)}) async-start(), calls=%async_computation.16 | async-start | bytes 1572864 | tf_op jit(solution)/shard_map/all_gather | solution.py:151
  10.6 273.4 %all-gather.19.cloned.1.call-start = ((), (), s32[]{:S(2)}) async-start(), calls=%async_computation.17 | async-start | bytes 1572864 | tf_op jit(solution)/shard_map/all_gather | solution.py:152
  11.8 385.4 %copy-start.55 = (f32[128]{0:T(128)}, f32[128]{0:T(128)S(1)}, u32[]{:S(2)}) copy-start(f32[128]{0:T(128)S(1)} %compare_convert_fusion) | copy-start | bytes 1540
  13.5 171.5 %copy-start.50 = (pred[128,128]{0,1:T(8,128)(4,1)}, pred[128,128]{0,1:T(8,128)(4,1)S(1)}, u32[]{:S(2)}) copy-start(pred[128,128]{0,1:T(8,128)(4,1)S(1)} %compare_and_fusion.1) | copy-start | bytes 49156
  57.1 127.1 %copy-start.29 = (f32[1024]{0:T(1024)}, f32[1024]{0:T(1024)S(1)}, u32[]{:S(2)}) copy-start(f32[1024]{0:T(1024)S(1)} %convert_element_type.150) | copy-start | bytes 12292
  58.2 126.0 %copy-start.47 = (f32[128]{0:T(128)}, f32[128]{0:T(128)S(1)}, u32[]{:S(2)}) copy-start(f32[128]{0:T(128)S(1)} %add_rsqrt_fusion.1) | copy-start | bytes 1540
  58.2 183.6 %copy-start.41 = (f32[1024]{0:T(1024)}, f32[1024]{0:T(1024)S(1)}, u32[]{:S(2)}) copy-start(f32[1024]{0:T(1024)S(1)} %convert_element_type.161) | copy-start | bytes 12292
  59.1 125.1 %copy-start.25 = (f32[128,32]{0,1:T(8,128)}, f32[128,32]{0,1:T(8,128)S(1)}, u32[]{:S(2)}) copy-start(f32[128,32]{0,1:T(8,128)S(1)} %get-tuple-element.41) | copy-start | bytes 49156
  59.2 333.1 %copy-start.39 = (f32[16,128]{1,0:T(8,128)}, f32[16,128]{1,0:T(8,128)S(1)}, u32[]{:S(2)}) copy-start(f32[16,128]{1,0:T(8,128)S(1)} %get-tuple-element.42) | copy-start | bytes 24580
  59.2 338.0 %copy-start.33 = (f32[128,16]{0,1:T(8,128)}, f32[128,16]{0,1:T(8,128)S(1)}, u32[]{:S(2)}) copy-start(f32[128,16]{0,1:T(8,128)S(1)} %get-tuple-element.43) | copy-start | bytes 24580
  69.3 115.7 %copy-start.19 = (bf16[128,512]{0,1:T(8,128)(2,1)}, bf16[128,512]{0,1:T(8,128)(2,1)S(1)}, u32[]{:S(2)}) copy-start(bf16[128,512]{0,1:T(8,128)(2,1)S(1)} %copy.69) | copy-start | bytes 393220
  125.1 59.5 %copy-start.35 = (bf16[128,8,32]{0,2,1:T(8,128)(2,1)}, bf16[128,8,32]{0,2,1:T(8,128)(2,1)S(1)}, u32[]{:S(2)}) copy-start(bf16[128,8,32]{0,2,1:T(8,128)(2,1)S(1)} %get-tuple-element.36) | copy-start | bytes 196612
  244.0 23.2 %all-to-all-start = ((bf16[16,24,1024]{2,1,0:T(8,128)(2,1)}), bf16[16,24,1024]{2,1,0:T(8,128)(2,1)S(1)}, u32[]{:S(2)}, u32[]{:S(2)}) async-start(bf16[16,24,1024]{2,1,0:T(8,128)(2,1)} %convolution_convert_fusion.4), calls=%async_computation | async-start | bytes 1572864 | tf_op jit(solution)/shard_map/all_to_all | solution.py:192
  248.5 58.3 %all-gather.21.cloned.1.call-start = ((), (), s32[]{:S(2)}) async-start(), calls=%async_computation.18 | async-start | bytes 1572864 | tf_op jit(solution)/shard_map/all_gather | solution.py:153
  306.8 85.0 %copy-start.12 = (bf16[128,1024]{1,0:T(8,128)(2,1)S(1)}, bf16[128,1024]{1,0:T(8,128)(2,1)}, u32[]{:S(2)}) copy-start(bf16[128,1024]{1,0:T(8,128)(2,1)} %param.17) | copy-start | bytes 786436
  309.6 82.3 %all-to-all-start.1 = ((bf16[16,24,1024]{2,1,0:T(8,128)(2,1)}), bf16[16,24,1024]{2,1,0:T(8,128)(2,1)S(1)}, u32[]{:S(2)}, u32[]{:S(2)}) async-start(bf16[16,24,1024]{2,1,0:T(8,128)(2,1)} %bitcast.18), calls=%async_computation.1 | async-start | bytes 1572864 | tf_op jit(solution)/shard_map/all_to_all | solution.py:195
  393.6 22.3 %all-to-all-start.2 = ((bf16[16,24,1024]{2,1,0:T(8,128)(2,1)}), bf16[16,24,1024]{2,1,0:T(8,128)(2,1)S(1)}, u32[]{:S(2)}, u32[]{:S(2)}) async-start(bf16[16,24,1024]{2,1,0:T(8,128)(2,1)} %multiply_convert_fusion), calls=%async_computation.2 | async-start | bytes 1572864 | tf_op jit(solution)/shard_map/all_to_all | solution.py:235
  397.2 140.4 %reduce-scatter.25.cloned.1.call-start = ((), (), s32[]{:S(2)}) async-start(), calls=%async_computation.26 | async-start | bytes 540672
  399.0 182.6 %reduce-scatter.19.cloned.1.call-start = ((), (), s32[]{:S(2)}) async-start(), calls=%async_computation.23 | async-start | bytes 1572864 | tf_op jit(solution)/shard_map/reduce_scatter | solution.py:308
  421.2 162.6 %reduce-scatter.21.cloned.1.call-start = ((), (), s32[]{:S(2)}) async-start(), calls=%async_computation.24 | async-start | bytes 1572864 | tf_op jit(solution)/shard_map/reduce_scatter | solution.py:311
  426.2 24.5 %all-to-all-start.3 = ((bf16[16,24,1024]{2,1,0:T(8,128)(2,1)}), bf16[16,24,1024]{2,1,0:T(8,128)(2,1)}, u32[]{:S(2)}, u32[]{:S(2)}) async-start(bf16[16,24,1024]{2,1,0:T(8,128)(2,1)} %bitcast.25), calls=%async_computation.3 | async-start | bytes 1572864 | tf_op jit(solution)/shard_map/all_to_all | solution.py:239
  432.0 170.9 %reduce-scatter.23.cloned.1.call-start = ((), (), s32[]{:S(2)}) async-start(), calls=%async_computation.25 | async-start | bytes 1572864 | tf_op jit(solution)/shard_map/reduce_scatter | solution.py:314
  442.1 302.8 %reduce-scatter.13.cloned.1.call-start = ((), (), s32[]{:S(2)}) async-start(), calls=%async_computation.20 | async-start | bytes 2162688 | tf_op jit(solution)/shard_map/reduce_scatter | solution.py:301
  459.5 422.8 %reduce-scatter.15.cloned.1.call-start = ((), (), s32[]{:S(2)}) async-start(), calls=%async_computation.21 | async-start | bytes 2162688 | tf_op jit(solution)/shard_map/reduce_scatter | solution.py:302
  463.5 561.6 %reduce-scatter.11.cloned.1.call-start = ((), (), s32[]{:S(2)}) async-start(), calls=%async_computation.19 | async-start | bytes 4325376 | tf_op jit(solution)/shard_map/reduce_scatter | solution.py:300
  468.6 699.5 %reduce-scatter.17.cloned.1.call-start = ((), (), s32[]{:S(2)}) async-start(), calls=%async_computation.22 | async-start | bytes 4325376 | tf_op jit(solution)/shard_map/reduce_scatter | solution.py:303
  472.3 66.7 %copy-start.1 = (bf16[1024,1024]{1,0:T(8,128)(2,1)S(1)}, bf16[1024,1024]{1,0:T(8,128)(2,1)}, u32[]{:S(2)}) copy-start(bf16[1024,1024]{1,0:T(8,128)(2,1)} %all-gather.13.cloned.1.call-done) | copy-start | bytes 6291460
  (44 other events, 425.9 us)
Sparse Core Ops, SparseCore 0:
  10.9 56.5 all-gather.8
  70.4 52.8 all-gather.10
  126.2 55.3 all-gather.12
  184.4 55.1 all-gather.14
  241.1 20.1 all-gather.16
  262.6 21.2 all-gather.18
  285.5 21.2 all-gather.20
  400.3 137.3 reduce-scatter.24
  540.4 17.0 reduce-scatter.18
  559.6 20.5 reduce-scatter.20
  582.4 20.4 reduce-scatter.22
  605.6 139.2 reduce-scatter.12
  747.7 134.5 reduce-scatter.14
  885.0 140.1 reduce-scatter.10
  1027.9 140.2 reduce-scatter.16
where the time goes:
time: 1180 us; the launch traced here: 1170 us
  waiting for transfers between devices  901 us (76%)
  blocking collectives  156 us (13%)
  matrix products  51.4 us (4%)
  starting transfers between devices  20 us (2%)
  other arithmetic  18.5 us (2%)
  between operations  14.8 us (1%)
  local copies, waits for them, and re-layouts  12.5 us (1%)
    reduce_scatter x1, waiting for transfers between devices, shards(): lax.psum_scatter(grad_w_output, ('dp', 'fsdp'), scatter_dimension=0, tile...  143 us
    reduce_scatter x1, waiting for transfers between devices, shards(): lax.psum_scatter(grad_w_query, ('dp', 'fsdp'), scatter_dimension=0, tiled...  143 us
    reduce_scatter x1, waiting for transfers between devices, shards(): lax.psum_scatter(grad_w_key, ('dp', 'fsdp'), scatter_dimension=0, tiled=T...  140 us
    reduce_scatter x1, waiting for transfers between devices, shards(): lax.psum_scatter(grad_w_value, ('dp', 'fsdp'), scatter_dimension=0, tiled...  137 us
    unnamed x2, blocking collectives  80 us
    all_gather x1, blocking collectives, shards(): lax.all_gather(router_weight, ('dp', 'fsdp'), axis=0, tiled=True)  76.2 us
    unnamed x16, waiting for transfers between devices  69.8 us
    all_gather x1, waiting for transfers between devices, shards(): lax.all_gather(query_weight, ('dp', 'fsdp'), axis=0, tiled=True)  56.5 us
  transfers between devices with their start and end apart: 19, of which 16 were waited for; matrix products, arithmetic and copies ran while one was open for 6% of the time, Pallas kernels for 0%

commit v1 on v0

--- a/solution.py
+++ b/solution.py
@@ -2,6 +2,7 @@
 import jax.numpy as jnp
 from jax import lax
 from jax.sharding import PartitionSpec as P
+from jax.lax import axis_index, ppermute, psum
 
 HEADS = 16
 KV_HEADS = 8
@@ -9,6 +10,24 @@
 TOP = 8
 CAP = 24
 norm_eps = 1e-05
+
+
+def try_all_pages(inner_x, dimension_no):
+    b_next = list(inner_x.shape[1:])
+    b_next[dimension_no] *= inner_x.shape[0]
+    return jnp.moveaxis(inner_x, 0, dimension_no).reshape(b_next)
+
+
+def convert_the_space(tile_in, axis_id):
+    nodes = psum(1, axis_id)
+    low = tile_in[None]
+    for j0 in range(nodes.bit_length() - 1):
+        t_next = 1 << j0
+        view_out = ppermute(low, axis_id, tuple(((ix, ix ^ t_next) for ix in range(nodes))))
+        near = jnp.stack([low, view_out], axis=0)
+        field_out = axis_index(axis_id) >> j0 & 1
+        low = jnp.where(field_out == 0, near, near[::-1]).reshape(-1, *tile_in.shape)
+    return low
 
 
 def positions_mask(doc_block):
@@ -135,6 +154,11 @@
     expert_up,
     expert_down,
 ):
+
+    def _store_records(inputs, patch, along_dim):
+        shaped = convert_the_space(inputs, patch)
+        return try_all_pages(shaped, along_dim)
+
     rows = hidden_in.shape[0]
     groups = HEADS // KV_HEADS
     scale = HEAD_DIM ** (-0.5)
@@ -145,7 +169,7 @@
         lax.all_gather(value_weight, ("dp", "fsdp"), axis=0, tiled=True),
         lax.all_gather(output_weight, ("dp", "fsdp"), axis=0, tiled=True),
         lax.all_gather(ffn_gain, ("dp", "fsdp"), axis=0, tiled=True),
-        lax.all_gather(router_weight, ("dp", "fsdp"), axis=0, tiled=True),
+        _store_records(router_weight, ("dp", "fsdp"), along_dim=0),
     )
     expert_full = (
         lax.all_gather(expert_gate, "fsdp", axis=1, tiled=True),

time: 1180 us -> 1120 us (0.949)
  waiting for transfers between devices: 901 us -> 842 us
    unnamed x16, waiting for transfers between devices: 69.8 us -> 3.83 us
    ppermute x0 -> x5, waiting for transfers between devices: none -> 21.3 us  [convert_the_space(): ppermute(low, axis_id, tuple(((ix, ix ^ t_next) for ix in range(nodes))))]
  transfers between devices with their start and end apart: 19 -> 24, of which waited for: 16 -> 19; matrix products, arithmetic and copies ran while one was open for 6% -> 7% of each run, Pallas kernels for 0% -> 0%
where the time goes in v1:
time: 1120 us
  waiting for transfers between devices  842 us (75%)
  blocking collectives  151 us (13%)
  matrix products  52.1 us (5%)
  starting transfers between devices  28.1 us (3%)
  other arithmetic  18.6 us (2%)
  between operations  15 us (1%)
  local copies, waits for them, and re-layouts  14.6 us (1%)
    reduce_scatter x1, waiting for transfers between devices, shards(): lax.psum_scatter(grad_w_output, ('dp', 'fsdp'), scatter_dimension=0, tile...  143 us
    reduce_scatter x1, waiting for transfers between devices, shards(): lax.psum_scatter(grad_w_query, ('dp', 'fsdp'), scatter_dimension=0, tiled...  142 us
    reduce_scatter x1, waiting for transfers between devices, shards(): lax.psum_scatter(grad_w_key, ('dp', 'fsdp'), scatter_dimension=0, tiled=T...  140 us
    reduce_scatter x1, waiting for transfers between devices, shards(): lax.psum_scatter(grad_w_value, ('dp', 'fsdp'), scatter_dimension=0, tiled...  138 us
    unnamed x2, blocking collectives  82.5 us
    all_gather x1, blocking collectives, shards(): lax.all_gather(router_weight, ('dp', 'fsdp'), axis=0, tiled=True)  68.5 us
    all_gather x1, waiting for transfers between devices, shards(): lax.all_gather(query_weight, ('dp', 'fsdp'), axis=0, tiled=True)  56.5 us
    all_gather x1, waiting for transfers between devices, shards(): lax.all_gather(output_weight, ('dp', 'fsdp'), axis=0, tiled=True)  54.4 us
  transfers between devices with their start and end apart: 24, of which 19 were waited for; matrix products, arithmetic and copies ran while one was open for 7% of the time, Pallas kernels for 0%

profile of v1, /device:TPU:0, one launch (start us, length us, event | category | flops | bytes accessed | tf_op | source)
XLA Modules:
  0.0 1121.9 jit_solution(7467553408258319338)
XLA Ops:
  15.2 41.9 %all-reduce.5 = (bf16[1024]{0:T(1024)(128)(2,1)S(1)}, bf16[1024]{0:T(1024)(128)(2,1)S(1)}) all-reduce(bf16[1024]{0:T(1024)(128)(2,1)S(1)} %dynamic-update-slice, bf16[1024]{0:T(1024)(128)(2,1)S(1)} %dynamic-update-slice.1), channel_id=1, replica_groups=mesh['dp'=16,'fsdp'=2] {'dp','fsdp'}, use_global_device_ids=true, to_apply=%add | all-reduce | flops 2048 | bytes 8192
  59.3 8.2 all-gather.9.cloned.1.call-done
  69.3 54.0 %all-gather.11.cloned.1.call-done = bf16[1024,512]{1,0:T(8,128)(2,1)} async-done(((bf16[32,512]{1,0:T(8,128)(2,1)}), bf16[1024,512]{1,0:T(8,128)(2,1)}) %all-gather.11.cloned.1.call-update) | async-done | bytes 1048592 | tf_op jit(solution)/shard_map/all_gather | solution.py:168
  125.2 56.5 %all-gather.13.cloned.1.call-done = bf16[1024,1024]{1,0:T(8,128)(2,1)} async-done(((bf16[32,1024]{1,0:T(8,128)(2,1)}), bf16[1024,1024]{1,0:T(8,128)(2,1)}) %all-gather.13.cloned.1.call-update) | async-done | bytes 2097168 | tf_op jit(solution)/shard_map/all_gather | solution.py:167
  185.2 54.4 %all-gather.15.cloned.1.call-done = bf16[1024,1024]{1,0:T(8,128)(2,1)} async-done(((bf16[32,1024]{1,0:T(8,128)(2,1)}), bf16[1024,1024]{1,0:T(8,128)(2,1)}) %all-gather.15.cloned.1.call-update) | async-done | bytes 2097168 | tf_op jit(solution)/shard_map/all_gather | solution.py:170
  244.0 4.5 all-to-all-start
  249.3 3.2 collective-permute-done
  255.7 5.6 all-gather.17.cloned.1.call-done
  261.3 5.8 all-to-all-done
  269.0 15.1 %all-gather.19.cloned.1.call-done = bf16[1,1024,512]{2,1,0:T(8,128)(2,1)} async-done(((bf16[1,512,512]{2,1,0:T(8,128)(2,1)}), bf16[1,1024,512]{2,1,0:T(8,128)(2,1)}) %all-gather.19.cloned.1.call-update) | async-done | bytes 1048592 | tf_op jit(solution)/shard_map/all_gather | solution.py:176
  284.0 2.7 multiply_convert_fusion.3
  286.7 20.2 %all-gather.21.cloned.1.call-done = bf16[1,512,1024]{2,1,0:T(8,128)(2,1)} async-done(((bf16[1,256,1024]{2,1,0:T(8,128)(2,1)}), bf16[1,512,1024]{2,1,0:T(8,128)(2,1)}) %all-gather.21.cloned.1.call-update) | async-done | bytes 1048592 | tf_op jit(solution)/shard_map/all_gather | solution.py:177
  306.9 2.7 convolution_convert_fusion.3
  309.6 5.8 all-to-all-start.1
  317.4 12.4 %collective-permute-done.3 = bf16[8,32,16]{1,0,2:T(8,128)(2,1)S(1)} collective-permute-done((bf16[8,32,16]{1,0,2:T(8,128)(2,1)S(1)}, bf16[8,32,16]{1,0,2:T(8,128)(2,1)S(1)}, u32[]{:S(2)}, u32[]{:S(2)}) %collective-permute-start.3) | collective-permute-done | bytes 8224 | tf_op jit(solution)/shard_map/ppermute | solution.py:26
  329.8 4.6 collective-permute-start.4
  334.4 4.6 collective-permute-done.4
  341.2 3.6 all-to-all-start.2
  346.7 16.8 %all-to-all-done.2 = bf16[16,24,1024]{2,1,0:T(8,128)(2,1)S(1)} async-done(((bf16[16,24,1024]{2,1,0:T(8,128)(2,1)}), bf16[16,24,1024]{2,1,0:T(8,128)(2,1)S(1)}, u32[]{:S(2)}, u32[]{:S(2)}) %all-to-all-start.2) | async-done | bytes 786464 | tf_op jit(solution)/shard_map/all_to_all | solution.py:259
  363.5 2.8 multiply_convert_fusion.1
  368.8 68.5 %all-gather = bf16[32,32,16]{1,2,0:T(8,128)(2,1)S(1)} all-gather(bf16[1,32,16]{1,2,0:T(8,128)(2,1)} %bitcast.192), channel_id=1, replica_groups=mesh['dp'=16,'fsdp'=2] {'dp','fsdp'}, dimensions={0}, use_global_device_ids=true | all-gather | bytes 33792 | tf_op jit(solution)/shard_map/all_gather | solution.py:240
  444.8 4.4 all-to-all-start.3
  451.1 4.1 gather_fusion
  459.3 8.6 all-to-all-done.3
  482.7 2.8 fusion.99
  486.4 2.7 fusion.56
  494.1 40.6 %all-reduce.4 = (f32[1024]{0:T(1024)S(1)}, f32[1024]{0:T(1024)S(1)}) all-reduce(f32[1024]{0:T(1024)S(1)} %get-tuple-element.14, f32[1024]{0:T(1024)S(1)} %get-tuple-element.12), channel_id=2, replica_groups=mesh['dp'=16,'fsdp'=2] {'dp','fsdp'}, use_global_device_ids=true, to_apply=%region_17.18.clone | all-reduce | flops 2048 | bytes 16384
  541.1 8.7 reduce-scatter.23.cloned.1.call-done
  551.9 139.9 %reduce-scatter.13.cloned.1.call-done = f32[32,512]{1,0:T(8,128)} async-done(((f32[1024,512]{1,0:T(8,128)}), f32[32,512]{1,0:T(8,128)}) %reduce-scatter.13.cloned.1.call-update) | async-done | bytes 65552 | tf_op jit(solution)/shard_map/reduce_scatter | solution.py:325
  691.8 137.9 %reduce-scatter.15.cloned.1.call-done = f32[32,512]{1,0:T(8,128)} async-done(((f32[1024,512]{1,0:T(8,128)}), f32[32,512]{1,0:T(8,128)}) %reduce-scatter.15.cloned.1.call-update) | async-done | bytes 65552 | tf_op jit(solution)/shard_map/reduce_scatter | solution.py:326
  829.7 142.4 %reduce-scatter.11.cloned.1.call-done = f32[32,1024]{1,0:T(8,128)} async-done(((f32[1024,1024]{1,0:T(8,128)}), f32[32,1024]{1,0:T(8,128)}) %reduce-scatter.11.cloned.1.call-update) | async-done | bytes 131088 | tf_op jit(solution)/shard_map/reduce_scatter | solution.py:324
  972.1 143.3 %reduce-scatter.17.cloned.1.call-done = f32[32,1024]{1,0:T(8,128)} async-done(((f32[1024,1024]{1,0:T(8,128)}), f32[32,1024]{1,0:T(8,128)}) %reduce-scatter.17.cloned.1.call-update) | async-done | bytes 131088 | tf_op jit(solution)/shard_map/reduce_scatter | solution.py:327
  (244 shorter events, 77.9 us)
Async XLA Ops:
  7.2 60.3 %all-gather.9.cloned.1.call-start = ((), (), s32[]{:S(2)}) async-start(), calls=%async_computation.12 | async-start | bytes 1081344 | tf_op jit(solution)/shard_map/all_gather | solution.py:169
  7.9 115.3 %all-gather.11.cloned.1.call-start = ((), (), s32[]{:S(2)}) async-start(), calls=%async_computation.13 | async-start | bytes 1081344 | tf_op jit(solution)/shard_map/all_gather | solution.py:168
  8.7 172.9 %all-gather.13.cloned.1.call-start = ((), (), s32[]{:S(2)}) async-start(), calls=%async_computation.14 | async-start | bytes 2162688 | tf_op jit(solution)/shard_map/all_gather | solution.py:167
  9.4 230.3 %all-gather.15.cloned.1.call-start = ((), (), s32[]{:S(2)}) async-start(), calls=%async_computation.15 | async-start | bytes 2162688 | tf_op jit(solution)/shard_map/all_gather | solution.py:170
  10.0 251.3 %all-gather.17.cloned.1.call-start = ((), (), s32[]{:S(2)}) async-start(), calls=%async_computation.16 | async-start | bytes 1572864 | tf_op jit(solution)/shard_map/all_gather | solution.py:175
  10.6 273.5 %all-gather.19.cloned.1.call-start = ((), (), s32[]{:S(2)}) async-start(), calls=%async_computation.17 | async-start | bytes 1572864 | tf_op jit(solution)/shard_map/all_gather | solution.py:176
  11.8 333.1 %copy-start.54 = (f32[128]{0:T(128)}, f32[128]{0:T(128)S(1)}, u32[]{:S(2)}) copy-start(f32[128]{0:T(128)S(1)} %compare_convert_fusion) | copy-start | bytes 1540
  13.5 171.2 %copy-start.49 = (pred[128,128]{0,1:T(8,128)(4,1)}, pred[128,128]{0,1:T(8,128)(4,1)S(1)}, u32[]{:S(2)}) copy-start(pred[128,128]{0,1:T(8,128)(4,1)S(1)} %compare_and_fusion.1) | copy-start | bytes 49156
  57.1 127.1 %copy-start.30 = (f32[1024]{0:T(1024)}, f32[1024]{0:T(1024)S(1)}, u32[]{:S(2)}) copy-start(f32[1024]{0:T(1024)S(1)} %convert_element_type.150) | copy-start | bytes 12292
  58.2 126.0 %copy-start.47 = (f32[128]{0:T(128)}, f32[128]{0:T(128)S(1)}, u32[]{:S(2)}) copy-start(f32[128]{0:T(128)S(1)} %add_rsqrt_fusion.1) | copy-start | bytes 1540
  58.2 183.7 %copy-start.41 = (f32[1024]{0:T(1024)}, f32[1024]{0:T(1024)S(1)}, u32[]{:S(2)}) copy-start(f32[1024]{0:T(1024)S(1)} %convert_element_type.161) | copy-start | bytes 12292
  59.1 125.1 %copy-start.26 = (f32[128,32]{0,1:T(8,128)}, f32[128,32]{0,1:T(8,128)S(1)}, u32[]{:S(2)}) copy-start(f32[128,32]{0,1:T(8,128)S(1)} %get-tuple-element.45) | copy-start | bytes 49156
  59.2 280.7 %copy-start.39 = (f32[16,128]{1,0:T(8,128)}, f32[16,128]{1,0:T(8,128)S(1)}, u32[]{:S(2)}) copy-start(f32[16,128]{1,0:T(8,128)S(1)} %get-tuple-element.46) | copy-start | bytes 24580
  59.2 285.7 %copy-start.32 = (f32[128,16]{0,1:T(8,128)}, f32[128,16]{0,1:T(8,128)S(1)}, u32[]{:S(2)}) copy-start(f32[128,16]{0,1:T(8,128)S(1)} %get-tuple-element.47) | copy-start | bytes 24580
  244.0 23.1 %all-to-all-start = ((bf16[16,24,1024]{2,1,0:T(8,128)(2,1)}), bf16[16,24,1024]{2,1,0:T(8,128)(2,1)S(1)}, u32[]{:S(2)}, u32[]{:S(2)}) async-start(bf16[16,24,1024]{2,1,0:T(8,128)(2,1)} %convolution_convert_fusion.4), calls=%async_computation | async-start | bytes 1572864 | tf_op jit(solution)/shard_map/all_to_all | solution.py:216
  248.5 58.4 %all-gather.21.cloned.1.call-start = ((), (), s32[]{:S(2)}) async-start(), calls=%async_computation.18 | async-start | bytes 1572864 | tf_op jit(solution)/shard_map/all_gather | solution.py:177
  248.6 3.9 collective-permute-start
  252.5 1.2 collective-permute-start.1
  253.7 61.6 %collective-permute-start.2 = (bf16[4,32,16]{1,2,0:T(8,128)(2,1)S(1)}, bf16[4,32,16]{1,2,0:T(8,128)(2,1)S(1)}, u32[]{:S(2)}, u32[]{:S(2)}) collective-permute-start(bf16[4,32,16]{1,2,0:T(8,128)(2,1)S(1)} %bitcast.188), channel_id=1, source_target_pairs={{0,4},{1,5},{2,6},{3,7},{4,0},{5,1},{6,2},{7,3},{8,12},{9,13},{10,... | collective-permute-start | bytes 12296 | tf_op jit(solution)/shard_map/ppermute | solution.py:26
  309.6 29.9 %all-to-all-start.1 = ((bf16[16,24,1024]{2,1,0:T(8,128)(2,1)}), bf16[16,24,1024]{2,1,0:T(8,128)(2,1)S(1)}, u32[]{:S(2)}, u32[]{:S(2)}) async-start(bf16[16,24,1024]{2,1,0:T(8,128)(2,1)} %bitcast.32), calls=%async_computation.1 | async-start | bytes 1572864 | tf_op jit(solution)/shard_map/all_to_all | solution.py:219
  315.4 14.4 %collective-permute-start.3 = (bf16[8,32,16]{1,0,2:T(8,128)(2,1)S(1)}, bf16[8,32,16]{1,0,2:T(8,128)(2,1)S(1)}, u32[]{:S(2)}, u32[]{:S(2)}) collective-permute-start(bf16[8,32,16]{1,0,2:T(8,128)(2,1)S(1)} %copy.77), channel_id=1, source_target_pairs={{0,8},{1,9},{2,10},{3,11},{4,12},{5,13},{6,14},{7,15},{8,0},{9,1},... | collective-permute-start | bytes 24584 | tf_op jit(solution)/shard_map/ppermute | solution.py:26
  329.8 9.2 collective-permute-start.4
  341.2 22.3 %all-to-all-start.2 = ((bf16[16,24,1024]{2,1,0:T(8,128)(2,1)}), bf16[16,24,1024]{2,1,0:T(8,128)(2,1)S(1)}, u32[]{:S(2)}, u32[]{:S(2)}) async-start(bf16[16,24,1024]{2,1,0:T(8,128)(2,1)} %multiply_convert_fusion), calls=%async_computation.2 | async-start | bytes 1572864 | tf_op jit(solution)/shard_map/all_to_all | solution.py:259
  344.8 144.4 %reduce-scatter.25.cloned.1.call-start = ((), (), s32[]{:S(2)}) async-start(), calls=%async_computation.26 | async-start | bytes 540672
  346.6 190.2 %reduce-scatter.19.cloned.1.call-start = ((), (), s32[]{:S(2)}) async-start(), calls=%async_computation.23 | async-start | bytes 1572864 | tf_op jit(solution)/shard_map/reduce_scatter | solution.py:332
  368.8 170.2 %reduce-scatter.21.cloned.1.call-start = ((), (), s32[]{:S(2)}) async-start(), calls=%async_computation.24 | async-start | bytes 1572864 | tf_op jit(solution)/shard_map/reduce_scatter | solution.py:335
  444.8 23.1 %all-to-all-start.3 = ((bf16[16,24,1024]{2,1,0:T(8,128)(2,1)}), bf16[16,24,1024]{2,1,0:T(8,128)(2,1)}, u32[]{:S(2)}, u32[]{:S(2)}) async-start(bf16[16,24,1024]{2,1,0:T(8,128)(2,1)} %bitcast.39), calls=%async_computation.3 | async-start | bytes 1572864 | tf_op jit(solution)/shard_map/all_to_all | solution.py:263
  449.2 100.6 %reduce-scatter.23.cloned.1.call-start = ((), (), s32[]{:S(2)}) async-start(), calls=%async_computation.25 | async-start | bytes 1572864 | tf_op jit(solution)/shard_map/reduce_scatter | solution.py:338
  459.3 232.5 %reduce-scatter.13.cloned.1.call-start = ((), (), s32[]{:S(2)}) async-start(), calls=%async_computation.20 | async-start | bytes 2162688 | tf_op jit(solution)/shard_map/reduce_scatter | solution.py:325
  476.4 353.3 %reduce-scatter.15.cloned.1.call-start = ((), (), s32[]{:S(2)}) async-start(), calls=%async_computation.21 | async-start | bytes 2162688 | tf_op jit(solution)/shard_map/reduce_scatter | solution.py:326
  480.4 491.7 %reduce-scatter.11.cloned.1.call-start = ((), (), s32[]{:S(2)}) async-start(), calls=%async_computation.19 | async-start | bytes 4325376 | tf_op jit(solution)/shard_map/reduce_scatter | solution.py:324
  485.5 629.9 %reduce-scatter.17.cloned.1.call-start = ((), (), s32[]{:S(2)}) async-start(), calls=%async_computation.22 | async-start | bytes 4325376 | tf_op jit(solution)/shard_map/reduce_scatter | solution.py:327
  (48 other events, 982.8 us)
Sparse Core Ops, SparseCore 0:
  10.9 56.5 all-gather.8
  70.4 52.8 all-gather.10
  126.2 55.3 all-gather.12
  184.4 55.1 all-gather.14
  241.1 20.2 all-gather.16
  262.7 21.2 all-gather.18
  285.6 21.2 all-gather.20
  347.9 136.7 reduce-scatter.24
  487.5 16.7 reduce-scatter.18
  506.4 20.6 reduce-scatter.20
  529.4 20.3 reduce-scatter.22
  552.5 139.2 reduce-scatter.12
  694.6 134.9 reduce-scatter.14
  832.4 139.6 reduce-scatter.10
  974.8 140.5 reduce-scatter.16
